TPU v7x, 512 devices: a whole 4x4x16 slice. The times are simulated.
512 devices in a mesh: half: 2 (over x_hi), quarter: 2 (over x_lo), grp: 128 (over y, z, core).
Axes of the slice: x: 4 (x_hi: 2, x_lo: 2; x = x_hi * 2 + x_lo), y: 4, z: 16, core: 2. Of those that a mesh axis runs over, the one named last changes fastest.
Arguments:
- rhs: float32 [131072, 512], P(('half', 'quarter', 'grp')), may hold values from -6 to 6
- left_one: float32 [131072, 128], P(('half', 'quarter', 'grp')), may hold values from -0.5 to 0.5
- left_two: float32 [131072, 128], P(('half', 'quarter', 'grp')), may hold values from -0.5 to 0.5
- middle_one: float32 [2, 128, 128, 128], P('half', 'grp'), may hold values from -0.5 to 0.5
- middle_two: float32 [4, 128, 128, 128], P(('half', 'quarter'), 'grp'), may hold values from -0.5 to 0.5
- right_one: float32 [131072, 128], P(('half', 'quarter', 'grp')), may hold values from -0.25 to 0.25
- right_two: float32 [131072, 128], P(('half', 'quarter', 'grp')), may hold values from -0.375 to 0.375
- order_one: int32 [2, 128, 128], P('half', 'grp'), may hold values from 0 to 127, each once within a row
- order_two: int32 [4, 128, 128], P(('half', 'quarter'), 'grp'), may hold values from 0 to 127, each once within a row
Outputs:
- product: float32 [131072, 512], P(('half', 'quarter', 'grp'))
Inputs may be any that keep to these rules, and one draw needn't show every extreme that they name: `order_one`: each row along the last dimension is a permutation of 0 .. 127. `order_two`: each row along the last dimension is a permutation of 0 .. 127.
All inputs are finite; a program needn't handle non-finite values.
Results may differ from a plain program's by a relative error of at most 0.000071.
Values sent between devices are 32-bit elements; how exact they have to be, the bound alone decides.
A program may use at most 64 MiB of HBM per device.

v0:
```python
import jax
import jax.numpy as jnp
from jax import lax
from jax.sharding import PartitionSpec as P


def from_everyone(array, axis):
    count = lax.axis_size(axis)
    return lax.all_to_all(
        jnp.broadcast_to(array[None], (count, *array.shape)), axis, 0, 0, tiled=True
    )


def over_copies(array, axis):
    return from_everyone(array, axis).sum(axis=0)


def swapped(value, axis, distance):
    mask = 2**distance
    pairs = [(source, source ^ mask) for source in range(lax.axis_size(axis))]
    return lax.ppermute(value, axis, pairs)


def matmul(left, right):
    return jnp.dot(left, right, precision=lax.Precision.HIGHEST, preferred_element_type=jnp.float32)


def project(factor, values):
    return lax.dot_general(
        factor,
        values,
        (((0,), (0,)), ((), ())),
        precision=lax.Precision.HIGHEST,
        preferred_element_type=jnp.float32,
    )


def to_slots(coeffs, order):
    groups = order.shape[0]
    parts = coeffs.reshape(groups, coeffs.shape[0] // groups, coeffs.shape[1])
    return jnp.take(parts, jnp.argsort(order), axis=0)


def on_device(
    rhs, left_one, left_two, middle_one, middle_two, right_one, right_two, order_one, order_two
):
    coeff_two = project(right_two, rhs)
    slots_two = to_slots(coeff_two, order_two[0, 0])
    partial_value = project(right_one, rhs)
    reduced = over_copies(partial_value, "quarter")
    slots_one = to_slots(reduced, order_one[0, 0])
    groups = slots_two.shape[0]
    part = slots_two.shape[1]
    folds = slots_two.shape[2] // slots_one.shape[2]
    width = slots_one.shape[2]
    folded = (
        slots_two.reshape(groups, part, folds, width)
        .transpose(0, 2, 1, 3)
        .reshape(groups, folds * part, width)
    )
    joined = jnp.concatenate([folded, slots_one], axis=1)
    split_rows = folds * part
    received = lax.all_to_all(joined, "grp", split_axis=0, concat_axis=0, tiled=True)
    count = received.shape[2]
    second = received[:, :split_rows].reshape(groups, folds, part, count)
    first = received[:, split_rows:].reshape(groups * part, count)
    second_sib = swapped(second, "quarter", 0)
    first_sib = swapped(first, "half", 0)
    outs_two = jnp.stack(
        [
            matmul(
                left_two, matmul(middle_two[0, 0], second_sib[:, 0].reshape(groups * part, count))
            )
        ],
        axis=0,
    )
    out_one = matmul(left_one, matmul(middle_one[0, 0], first_sib))
    outs_two, level_stack = (outs_two, out_one[None])
    result_two = outs_two[0]
    result_one = level_stack[0]
    return result_one + result_two


def solution(mesh):
    in_specs = (
        P(("half", "quarter", "grp"), None),
        P(("half", "quarter", "grp"), None),
        P(("half", "quarter", "grp"), None),
        P("half", "grp", None, None),
        P(("half", "quarter"), "grp", None, None),
        P(("half", "quarter", "grp"), None),
        P(("half", "quarter", "grp"), None),
        P("half", "grp", None),
        P(("half", "quarter"), "grp", None),
    )
    out_specs = P(("half", "quarter", "grp"), None)
    return jax.shard_map(
        on_device, mesh=mesh, in_specs=in_specs, out_specs=out_specs, check_vma=False
    )
```

profile of v0, /device:TPU:1, one launch (start us, length us, event | category | flops | bytes accessed | tf_op | source)
XLA Modules:
  0.0 88.9 jit_solution(11448268040225401951)
XLA Ops:
  0.0 0.0 copy-start
  0.0 1.0 %copy-done = f32[256,512]{1,0:T(8,128)S(1)} copy-done((f32[256,512]{1,0:T(8,128)S(1)}, f32[256,512]{1,0:T(8,128)}, u32[]{:S(2)}) %copy-start) | copy-done | bytes 524312
  1.0 1.4 %fusion.8 = f32[128,512]{1,0:T(8,128)S(1)} fusion(f32[256,128]{1,0:T(8,128)} %param.16, f32[256,512]{1,0:T(8,128)S(1)} %copy-done), kind=kOutput, calls=%fused_computation.22 | convolution fusion | flops 201326592 | bytes 917504 | tf_op jit(solution)/shard_map/dot_general | solution.py:29
  2.4 0.9 broadcast_in_dim.15
  3.3 0.0 copy-start.1
  3.3 3.6 %all-to-all-start = ((f32[2,128,512]{2,1,0:T(8,128)}), f32[2,128,512]{2,1,0:T(8,128)S(1)}, u32[]{:S(2)}, u32[]{:S(2)}) async-start(f32[2,128,512]{2,1,0:T(8,128)} %broadcast_in_dim.15), calls=%async_computation | async-start | bytes 1048576 | tf_op jit(solution)/shard_map/all_to_all | solution.py:9
  6.9 0.0 copy-start.6
  6.9 0.6 copy-done.6
  7.5 2.6 %sort.32 = (s32[128]{0:T(128)}, s32[128]{0:T(128)S(1)}) sort(s32[128]{0:T(128)S(1)} %bitcast.34, s32[128]{0:T(128)S(1)} %iota.8), dimensions={0}, to_apply=%region_2.4 | sort | flops 896 | bytes 2048 | tf_op jit(solution)/shard_map/jit(argsort)/sort | solution.py:41
  10.2 0.0 copy-done.1
  10.2 0.5 fusion.7
  10.7 0.0 copy-start.7
  10.7 0.6 copy-done.7
  11.3 2.6 %sort.31 = (s32[128]{0:T(128)}, s32[128]{0:T(128)S(1)}) sort(s32[128]{0:T(128)S(1)} %bitcast.35, s32[128]{0:T(128)S(1)} %iota.7), dimensions={0}, to_apply=%region_0.0 | sort | flops 896 | bytes 2048 | tf_op jit(solution)/shard_map/jit(argsort)/sort | solution.py:41
  13.9 0.8 gather_fusion
  14.7 0.0 all-to-all-done
  14.8 0.8 gather_fusion.1
  15.5 0.1 bitcast_select_fusion
  15.7 0.4 copy.13
  16.1 53.9 %all_to_all.10 = f32[128,2,512]{2,1,0:T(2,128)S(1)} all-to-all(f32[128,2,512]{2,1,0:T(2,128)S(1)} %copy.13), channel_id=1, replica_groups=mesh['half'=2,'quarter'=2,'grp'=128] {'grp'}, dimensions={0} | all-to-all | bytes 1048576 | tf_op jit(solution)/shard_map/all_to_all | solution.py:63
  70.1 0.4 slice_bitcast_fusion
  70.5 0.0 copy-start.4
  70.5 4.7 %collective-permute-start = (f32[128,512]{1,0:T(8,128)S(1)}, f32[128,512]{1,0:T(8,128)S(1)}, u32[]{:S(2)}, u32[]{:S(2)}) collective-permute-start(f32[128,512]{1,0:T(8,128)S(1)} %bitcast.33), channel_id=1, source_target_pairs={{0,256},{256,0},{1,257},{257,1},{2,258},{258,2},{3,259},{259,3},{4... | collective-permute-start | bytes 786440 | tf_op jit(solution)/shard_map/ppermute | solution.py:21
  75.2 0.0 copy-start.2
  75.2 2.8 %collective-permute-start.1 = (f32[128,1,1,512]{3,1,2,0:T(1,128)S(1)}, f32[128,1,1,512]{3,1,2,0:T(1,128)S(1)}, u32[]{:S(2)}, u32[]{:S(2)}) collective-permute-start(f32[128,1,1,512]{3,1,2,0:T(1,128)S(1)} %get-tuple-element.10), channel_id=1, source_target_pairs={{0,128},{128,0},{1,129},{129,1},{2,130},{130,2},{3,131},{131,3},{4... | collective-permute-start | bytes 786440 | tf_op jit(solution)/shard_map/ppermute | solution.py:21
  77.9 2.6 %collective-permute-done = f32[128,512]{1,0:T(8,128)S(1)} collective-permute-done((f32[128,512]{1,0:T(8,128)S(1)}, f32[128,512]{1,0:T(8,128)S(1)}, u32[]{:S(2)}, u32[]{:S(2)}) %collective-permute-start) | collective-permute-done | bytes 262176 | tf_op jit(solution)/shard_map/ppermute | solution.py:21
  80.6 0.0 copy-done.4
  80.6 0.6 fusion.5
  81.2 0.0 copy-done.2
  81.2 0.0 copy-start.5
  81.2 0.6 fusion.9
  81.8 0.0 copy-start.3
  81.8 4.9 %collective-permute-done.1 = f32[128,1,1,512]{3,1,2,0:T(1,128)S(1)} collective-permute-done((f32[128,1,1,512]{3,1,2,0:T(1,128)S(1)}, f32[128,1,1,512]{3,1,2,0:T(1,128)S(1)}, u32[]{:S(2)}, u32[]{:S(2)}) %collective-permute-start.1) | collective-permute-done | bytes 262176 | tf_op jit(solution)/shard_map/ppermute | solution.py:21
  86.7 0.0 copy-done.5
  86.7 0.6 fusion.1
  87.3 0.0 copy-done.3
  87.3 0.6 fusion
  87.9 1.0 %copy.14 = f32[256,512]{1,0:T(8,128)} copy(f32[256,512]{0,1:T(8,128)S(1)} %fusion) | data formatting | bytes 1048576 | tf_op jit(solution)/shard_map/add | solution.py:81
  (11 shorter events, 0.1 us)
Async XLA Ops:
  0.0 1.0 %copy-start = (f32[256,512]{1,0:T(8,128)S(1)}, f32[256,512]{1,0:T(8,128)}, u32[]{:S(2)}) copy-start(f32[256,512]{1,0:T(8,128)} %param.11) | copy-start | bytes 1572868
  3.3 6.9 %copy-start.1 = (f32[256,128]{1,0:T(8,128)S(1)}, f32[256,128]{1,0:T(8,128)}, u32[]{:S(2)}) copy-start(f32[256,128]{1,0:T(8,128)} %param.17) | copy-start | bytes 393220
  3.3 11.5 %all-to-all-start = ((f32[2,128,512]{2,1,0:T(8,128)}), f32[2,128,512]{2,1,0:T(8,128)S(1)}, u32[]{:S(2)}, u32[]{:S(2)}) async-start(f32[2,128,512]{2,1,0:T(8,128)} %broadcast_in_dim.15), calls=%async_computation | async-start | bytes 1048576 | tf_op jit(solution)/shard_map/all_to_all | solution.py:9
  6.9 0.7 copy-start.6
  10.7 0.7 copy-start.7
  70.5 10.1 %copy-start.4 = (f32[1,1,128,128]{3,2,1,0:T(8,128)S(1)}, f32[1,1,128,128]{3,2,1,0:T(8,128)}, u32[]{:S(2)}) copy-start(f32[1,1,128,128]{3,2,1,0:T(8,128)} %param.14) | copy-start | bytes 196612
  70.5 10.1 %collective-permute-start = (f32[128,512]{1,0:T(8,128)S(1)}, f32[128,512]{1,0:T(8,128)S(1)}, u32[]{:S(2)}, u32[]{:S(2)}) collective-permute-start(f32[128,512]{1,0:T(8,128)S(1)} %bitcast.33), channel_id=1, source_target_pairs={{0,256},{256,0},{1,257},{257,1},{2,258},{258,2},{3,259},{259,3},{4... | collective-permute-start | bytes 786440 | tf_op jit(solution)/shard_map/ppermute | solution.py:21
  75.2 6.0 %copy-start.2 = (f32[256,128]{1,0:T(8,128)S(1)}, f32[256,128]{1,0:T(8,128)}, u32[]{:S(2)}) copy-start(f32[256,128]{1,0:T(8,128)} %param.12) | copy-start | bytes 393220
  75.2 11.5 %collective-permute-start.1 = (f32[128,1,1,512]{3,1,2,0:T(1,128)S(1)}, f32[128,1,1,512]{3,1,2,0:T(1,128)S(1)}, u32[]{:S(2)}, u32[]{:S(2)}) collective-permute-start(f32[128,1,1,512]{3,1,2,0:T(1,128)S(1)} %get-tuple-element.10), channel_id=1, source_target_pairs={{0,128},{128,0},{1,129},{129,1},{2,130},{130,2},{3,131},{131,3},{4... | collective-permute-start | bytes 786440 | tf_op jit(solution)/shard_map/ppermute | solution.py:21
  81.2 5.5 %copy-start.5 = (f32[1,1,128,128]{3,2,1,0:T(8,128)S(1)}, f32[1,1,128,128]{3,2,1,0:T(8,128)}, u32[]{:S(2)}) copy-start(f32[1,1,128,128]{3,2,1,0:T(8,128)} %param.15) | copy-start | bytes 196612
  81.8 5.5 %copy-start.3 = (f32[256,128]{1,0:T(8,128)S(1)}, f32[256,128]{1,0:T(8,128)}, u32[]{:S(2)}) copy-start(f32[256,128]{1,0:T(8,128)} %param.13) | copy-start | bytes 393220
where the time goes:
time: 89.4 us; the launch traced here: 88.9 us
  blocking collectives  53.9 us (60%)
  starting transfers between devices  11 us (12%)
  waiting for transfers between devices  7.54 us (8%)
  local copies, waits for them, and re-layouts  6.55 us (7%)
  other arithmetic  5.44 us (6%)
  matrix products  4.14 us (5%)
    all_to_all x1, blocking collectives, on_device(): lax.all_to_all(joined, 'grp', split_axis=0, concat_axis=0, tiled=True)  53.9 us
    ppermute x2, waiting for transfers between devices, swapped(): return lax.ppermute(value, axis, pairs)  7.53 us
    ppermute x2, starting transfers between devices, swapped(): return lax.ppermute(value, axis, pairs)  7.42 us
    sort x2, other arithmetic, to_slots(): return jnp.take(parts, jnp.argsort(order), axis=0)  5.23 us
    all_to_all x1, starting transfers between devices, from_everyone(): lax.all_to_all(jnp.broadcast_to(array[None], (count, *array.shape)), axis...  3.62 us
    unnamed x17, local copies, waits for them, and re-layouts  2.37 us
    dot_general x4, matrix products, matmul(): jnp.dot(left, right, precision=lax.Precision.HIGHEST, preferred_element_t...  2.33 us
    dot_general x2, matrix products, project(): lax.dot_general(factor, values, (((0,), (0,)), ((), ())), precision=lax.P...  1.81 us
  transfers between devices with their start and end apart: 3, of which 2 were waited for; matrix products, arithmetic and copies ran while one was open for 9% of the time, Pallas kernels for 0%

commit v1 on v0

v1 whole, which is shorter than its diff:
```python
import functools

import jax
import jax.numpy as jnp
from jax import lax
from jax.experimental import pallas as pl
from jax.experimental.pallas import tpu as pltpu
from jax.sharding import PartitionSpec as P

MESH = pl.DeviceIdType.MESH
G = 128
HALF = 64
NZ = 16
NY = 4
BF = jnp.bfloat16
F32 = jnp.float32


def split(a):
    high = a.astype(BF)
    return high, (a - high.astype(F32)).astype(BF)


def dot(a, b, dims=(((1,), (0,)), ((), ()))):
    return lax.dot_general(a, b, dims, preferred_element_type=F32)


def dot3(a, b):
    (ah, al), (bh, bl) = a, b
    return dot(ah, bh) + (dot(ah, bl) + dot(al, bh))


def permuted(factor, order, slot):
    hot = (order == slot).astype(F32).astype(BF)
    high, low = split(factor)
    nt = (((1,), (1,)), ((), ()))
    return dot(hot, high, nt).astype(BF), dot(hot, low, nt).astype(BF)


def kernel(
    x_hbm, l1_hbm, l2_hbm, m1_hbm, m2_hbm, rr1_hbm, rr2_hbm, o1_hbm, o2_hbm, out_hbm,
    x, l1, l2, m1, m2, rr1, rr2, o1, o2, out,
    s2, p1, in1, s1, r2, r1,
    load_sem, send2, recv2, xs, xr, send1, recv1, fs, fr, out_sem, stage_b, stage_c,
):
    h = lax.axis_index("half")
    q = lax.axis_index("quarter")
    me = lax.axis_index("grp")
    y, z, c = me // (2 * NZ), (me // 2) % NZ, me % 2

    loads = []
    for n, (a, b) in enumerate((
        (x_hbm, x), (rr2_hbm, rr2), (o2_hbm.at[0], o2), (rr1_hbm, rr1), (o1_hbm.at[0], o1),
        (m2_hbm.at[0, 0], m2), (m1_hbm.at[0, 0], m1), (l2_hbm, l2), (l1_hbm, l1),
    )):
        loads.append(pltpu.make_async_copy(a, b, load_sem.at[n]))

    def plane(s):
        t = (y * 2 + c + s) % (2 * NY)
        return {"half": h, "quarter": q, "grp": ((t // 2) * NZ + z) * 2 + t % 2}

    def across(s):
        t = (h * 2 + q) ^ s
        return {"half": t // 2, "quarter": t % 2, "grp": me}

    def column(s):
        return {"half": h, "quarter": q, "grp": (y * NZ + (z + s) % NZ) * 2 + c}

    barrier = pltpu.get_barrier_semaphore()
    for s in range(1, NZ):
        pl.semaphore_signal(barrier, inc=1, device_id=column(s), device_id_type=MESH)
    for s in range(1, 2 * NY):
        pl.semaphore_signal(barrier, inc=1, device_id=plane(s), device_id_type=MESH)
    for s in range(1, 4):
        pl.semaphore_signal(barrier, inc=1, device_id=across(s), device_id_type=MESH)
    for copy in loads:
        copy.start()

    slot2 = lax.broadcasted_iota(jnp.int32, (G, G), 0)
    slot1 = (slot2 % HALF) * 2 + slot2 // HALF
    loads[0].wait()
    xs_ = split(x[...])
    loads[1].wait()
    loads[2].wait()
    c2 = dot3(permuted(rr2[...], o2[...], slot2), xs_)
    for k in range(4):
        s2[:, k, :] = c2[:, 128 * k : 128 * k + 128]
    loads[3].wait()
    loads[4].wait()
    c1 = dot3(permuted(rr1[...], o1[...], slot1), xs_)
    for e in range(2):
        for k in range(4):
            p1[e, :, k, :] = c1[HALF * e : HALF * e + HALF, 128 * k : 128 * k + 128]

    pl.semaphore_wait(barrier, (NZ - 1) + (2 * NY - 1) + 3)
    for s in range(1, 2 * NY):
        pl.semaphore_signal(stage_b, inc=1, device_id=plane(s), device_id_type=MESH)
    part = pltpu.make_async_remote_copy(
        p1.at[1 - q], in1, xs, xr, device_id=across(1), device_id_type=MESH)
    part.start()
    pl.semaphore_wait(stage_b, 2 * NY - 1)
    for s in range(1, 4):
        pl.semaphore_signal(stage_c, inc=1, device_id=across(s), device_id_type=MESH)
    pl.semaphore_wait(stage_c, 3)

    def level_two(s, carry):
        d = (me + s) % G
        pltpu.make_async_remote_copy(
            s2.at[d], r2.at[me], send2, recv2,
            device_id={"half": h, "quarter": 1 - q, "grp": d}, device_id_type=MESH).start()
        return carry

    lax.fori_loop(0, 48, level_two, 0)

    part.wait()
    s1[...] = p1[q] + in1[...]

    def level_one(s, carry):
        k = (me // 2 + s) % HALF
        pltpu.make_async_remote_copy(
            s1.at[k], r1.at[me], send1, recv1,
            device_id={"half": 1 - h, "quarter": 1 - q, "grp": k * 2 + q}, device_id_type=MESH).start()
        return carry

    lax.fori_loop(0, HALF, level_one, 0)
    lax.fori_loop(48, G, level_two, 0)

    for copy in loads[5:]:
        copy.wait()
    m2s, m1s, l2s, l1s = split(m2[...]), split(m1[...]), split(l2[...]), split(l1[...])

    first = c == 1 - q
    forward = pltpu.make_async_remote_copy(
        r1, r1, fs, fr, device_id=across(1), device_id_type=MESH)
    rows1 = pltpu.make_async_remote_copy(
        r1, r1, send1, recv1, device_id=across(1), device_id_type=MESH)
    rows2 = pltpu.make_async_remote_copy(
        s2, r2, send2, recv2, device_id=across(1), device_id_type=MESH)
    sent1 = pltpu.make_async_remote_copy(
        s1, s1, send1, recv1, device_id=across(1), device_id_type=MESH)

    @pl.when(first)
    def _():
        rows1.wait_recv()
        forward.start()

    rows2.wait_recv()
    parts = []
    for k in range(4):
        w2 = split(dot3(m2s, split(r2[:, k, :])))
        parts.append(dot3(l2s, w2))

    @pl.when(jnp.logical_not(first))
    def _():
        forward.wait_recv()

    stores = []
    for k in range(4):
        w1 = split(dot3(m1s, split(r1[:, k, :])))
        out[:, 128 * k : 128 * k + 128] = parts[k] + dot3(l1s, w1)
    store = pltpu.make_async_copy(out, out_hbm, out_sem)
    store.start()

    @pl.when(first)
    def _():
        forward.wait_send()

    rows2.wait_send()
    sent1.wait_send()
    store.wait()


def on_device(rhs, left_one, left_two, middle_one, middle_two, right_one, right_two, order_one, order_two):
    dma = pltpu.SemaphoreType.DMA
    any_space = pl.BlockSpec(memory_space=pl.ANY)
    return pl.pallas_call(
        kernel,
        out_shape=jax.ShapeDtypeStruct((256, 512), F32),
        in_specs=[any_space] * 9,
        out_specs=any_space,
        scratch_shapes=[
            pltpu.VMEM((256, 512), F32),
            pltpu.VMEM((256, 128), F32),
            pltpu.VMEM((256, 128), F32),
            pltpu.VMEM((128, 128), F32),
            pltpu.VMEM((128, 128), F32),
            pltpu.VMEM((256, 128), F32),
            pltpu.VMEM((256, 128), F32),
            pltpu.VMEM((1, 128), jnp.int32),
            pltpu.VMEM((1, 128), jnp.int32),
            pltpu.VMEM((256, 512), F32),
            pltpu.VMEM((G, 4, 128), F32),
            pltpu.VMEM((2, HALF, 4, 128), F32),
            pltpu.VMEM((HALF, 4, 128), F32),
            pltpu.VMEM((HALF, 4, 128), F32),
            pltpu.VMEM((G, 4, 128), F32),
            pltpu.VMEM((G, 4, 128), F32),
            dma((9,)), dma, dma, dma, dma, dma, dma, dma, dma, dma,
            pltpu.SemaphoreType.REGULAR,
            pltpu.SemaphoreType.REGULAR,
        ],
        compiler_params=pltpu.CompilerParams(collective_id=0, has_side_effects=True),
        name="butterfly",
    )(rhs, left_one, left_two, middle_one, middle_two, right_one, right_two, order_one, order_two)


def solution(mesh):
    rows = P(("half", "quarter", "grp"), None)
    in_specs = (
        rows, rows, rows,
        P("half", "grp", None, None),
        P(("half", "quarter"), "grp", None, None),
        rows, rows,
        P("half", "grp", None),
        P(("half", "quarter"), "grp", None),
    )
    return jax.shard_map(on_device, mesh=mesh, in_specs=in_specs, out_specs=rows, check_vma=False)
```

time: 89.4 us -> 46.9 us (0.52)
  blocking collectives: 53.9 us -> 0 us
  Pallas kernels: 0 us -> 44.9 us
  starting transfers between devices: 11 us -> 0 us
  waiting for transfers between devices: 7.54 us -> 0 us
  other arithmetic: 5.44 us -> 0 us
  local copies, waits for them, and re-layouts: 6.55 us -> 1.87 us
  matrix products: 4.14 us -> 0 us
    all_to_all x1 -> x0, blocking collectives: 53.9 us -> none  [on_device(): lax.all_to_all(joined, 'grp', split_axis=0, concat_axis=0, tiled=True)]
    pallas_call x0 -> x1, Pallas kernels: none -> 44.9 us  [on_device(): pl.pallas_call(kernel, out_shape=jax.ShapeDtypeStruct((256, 512), F32), i...]
    ppermute x2 -> x0, waiting for transfers between devices: 7.53 us -> none  [swapped(): return lax.ppermute(value, axis, pairs)]
    ppermute x2 -> x0, starting transfers between devices: 7.42 us -> none  [swapped(): return lax.ppermute(value, axis, pairs)]
    sort x2 -> x0, other arithmetic: 5.23 us -> none  [to_slots(): return jnp.take(parts, jnp.argsort(order), axis=0)]
    dot_general x6 -> x0, matrix products: 4.14 us -> none  [the longest x4 2.33 us: matmul(): jnp.dot(left, right, precision=lax.Precision.HIGHEST, preferred_element_t...]
    all_to_all x1 -> x0, starting transfers between devices: 3.62 us -> none  [from_everyone(): lax.all_to_all(jnp.broadcast_to(array[None], (count, *array.shape)), axis...]
    gather x2 -> x0, local copies, waits for them, and re-layouts: 1.51 us -> none  [to_slots(): return jnp.take(parts, jnp.argsort(order), axis=0)]
  transfers between devices with their start and end apart: 3 -> 0, of which waited for: 2 -> 0; matrix products, arithmetic and copies ran while one was open for 9% -> 0% of each run, Pallas kernels for 0% -> 0%
where the time goes in v1:
time: 46.9 us; the launch traced here: 46.7 us
  Pallas kernels  44.9 us (96%)
  local copies, waits for them, and re-layouts  1.87 us (4%)
    pallas_call x1, Pallas kernels, on_device(): pl.pallas_call(kernel, out_shape=jax.ShapeDtypeStruct((256, 512), F32), i...  44.9 us
    unnamed x1, local copies, waits for them, and re-layouts  1.87 us

profile of v1, /device:TPU:1, one launch (start us, length us, event | category | flops | bytes accessed | tf_op | source)
XLA Modules:
  0.0 46.7 jit_solution(3957873486504640511)
XLA Ops:
  0.0 44.9 %butterfly.1 = f32[256,512]{1,0:T(8,128)} custom-call(f32[256,512]{1,0:T(8,128)} %x_hbm.1, f32[256,128]{1,0:T(8,128)} %l1_hbm.1, f32[256,128]{1,0:T(8,128)} %l2_hbm.1, f32[1,1,128,128]{3,2,1,0:T(8,128)} %m1_hbm.1, f32[1,1,128,128]{3,2,1,0:T(8,128)} %m2_hbm.1, f32[256,128]{1,0:T(8,128)} %rr1_hbm.1, f32[256,128]{1,0:T(8,128)} %rr2_hbm.1, s32[1,1,128]{2,1,0:T(1,128)} %o1_hbm.1, ...), custom_call_target="tpu_custom_call" | custom-call | tf_op jit(solution)/shard_map/butterfly/pallas_call | solution.py:176
  44.9 1.9 %copy.11 = f32[256,512]{1,0:T(8,128)} copy(f32[256,512]{1,0:T(8,128)} %butterfly.1) | data formatting | bytes 1048576

commit v2 on v1

v2 whole, which is shorter than its diff:
```python
import functools

import jax
import jax.numpy as jnp
from jax import lax
from jax.experimental import pallas as pl
from jax.experimental.pallas import tpu as pltpu
from jax.sharding import PartitionSpec as P

MESH = pl.DeviceIdType.MESH
G = 128
HALF = 64
NZ = 16
NY = 4
BF = jnp.bfloat16
F32 = jnp.float32


def split(a):
    high = a.astype(BF)
    return high, (a - high.astype(F32)).astype(BF)


def dot(a, b, dims=(((1,), (0,)), ((), ()))):
    return lax.dot_general(a, b, dims, preferred_element_type=F32)


def dot3(a, b):
    (ah, al), (bh, bl) = a, b
    return dot(ah, bh) + (dot(ah, bl) + dot(al, bh))


def permuted(factor, order, slot):
    hot = (order == slot).astype(F32).astype(BF)
    high, low = split(factor)
    nt = (((1,), (1,)), ((), ()))
    return dot(hot, high, nt).astype(BF), dot(hot, low, nt).astype(BF)


NEAR = (4, -4, 3, -3, 2, -2, 1, -1)
FAR = (8, 7, -7, 6, -6, 5, -5)


def kernel(
    x_hbm, l1_hbm, l2_hbm, m1_hbm, m2_hbm, rr1_hbm, rr2_hbm, o1_hbm, o2_hbm, out,
    x, l1, l2, m1, m2, rr1, rr2, o1, o2,
    s2, p1, in1, s1, z2, r2, r1,
    load_sem, zs2, zr2, xs, xr, zs1, zr1, send2, recv2, fs, fr, stage, opposite_in,
):
    h = lax.axis_index("half")
    q = lax.axis_index("quarter")
    me = lax.axis_index("grp")
    y, z, c = me // (2 * NZ), (me // 2) % NZ, me % 2
    yc = y * 2 + c

    loads = []
    for n, (a, b) in enumerate((
        (x_hbm, x), (rr2_hbm, rr2), (o2_hbm.at[0], o2), (rr1_hbm, rr1), (o1_hbm.at[0], o1),
        (m2_hbm.at[0, 0], m2), (m1_hbm.at[0, 0], m1), (l2_hbm, l2), (l1_hbm, l1),
    )):
        loads.append(pltpu.make_async_copy(a, b, load_sem.at[n]))

    def signal(semaphore, device):
        pl.semaphore_signal(semaphore, inc=1, device_id=device, device_id_type=MESH)

    def place(zz, t):
        return ((t // 2) * NZ + zz) * 2 + t % 2

    def level(dz):
        return (z + dz + NZ) % NZ

    def column(dz):
        return {"half": h, "quarter": q, "grp": place(level(dz), yc)}

    def sibling(dz):
        return {"half": h, "quarter": 1 - q, "grp": place(level(dz), yc)}

    across = {"half": h, "quarter": 1 - q, "grp": me}
    opposite = {"half": 1 - h, "quarter": q, "grp": me}

    for copy in loads:
        copy.start()
    barrier = pltpu.get_barrier_semaphore()
    for dz in NEAR:
        signal(barrier, sibling(dz))
    for dz in (4, -4):
        signal(barrier, column(dz))
    signal(barrier, opposite)
    for s in range(1, 16):
        t = (yc * 2 + q + s) % 16
        signal(barrier, {"half": h, "quarter": t % 2, "grp": place(z, t // 2)})

    i = lax.broadcasted_iota(jnp.int32, (G, G), 0)
    slot2 = (((i // 2) % 4) * NZ + i // 8) * 2 + i % 2
    slot1 = ((i // 32) * NZ + i % NZ) * 2 + (i // NZ) % 2
    loads[0].wait()
    xs_ = split(x[...])
    loads[1].wait()
    loads[2].wait()
    c2 = dot3(permuted(rr2[...], o2[...], slot2), xs_)
    for k in range(4):
        s2[:, k, :] = c2[:, 128 * k : 128 * k + 128]
    loads[3].wait()
    loads[4].wait()
    c1 = dot3(permuted(rr1[...], o1[...], slot1), xs_)
    for k in range(4):
        p1[:, k, :] = c1[:, 128 * k : 128 * k + 128]

    def along_two(dz):
        return pltpu.make_async_remote_copy(
            s2.at[pl.ds(level(dz) * 8, 8)], z2.at[-dz % NZ], zs2, zr2.at[-dz % NZ],
            device_id=sibling(dz), device_id_type=MESH)

    def spread_two(first, count):
        for zi in range(first, first + count):
            along_two(-zi).wait_recv()

        def send(n, carry):
            t = (yc + n) % 8
            pltpu.make_async_remote_copy(
                z2.at[pl.ds(first, count), t], r2.at[pl.ds(yc * NZ + first, count)], send2, recv2,
                device_id={"half": h, "quarter": q, "grp": place(z, t)}, device_id_type=MESH).start()
            return carry

        lax.fori_loop(1, 8, send, 0)

    alone = c == q

    def spread_one(n, carry):
        t = (yc + n) % 8
        pltpu.make_async_remote_copy(
            p1.at[pl.ds(t * NZ, NZ)], in1.at[q * 4 + y], xs, xr,
            device_id={"half": h, "quarter": c, "grp": place(z, t)}, device_id_type=MESH).start()
        return carry

    def along_one(dz):
        return pltpu.make_async_remote_copy(
            s1.at[:, level(dz)], r1.at[q, -dz % NZ], zs1, zr1.at[-dz % NZ],
            device_id={"half": 1 - h, "quarter": 1 - q, "grp": place(level(dz), yc)},
            device_id_type=MESH)

    def whole(a, b, sent, received):
        return pltpu.make_async_remote_copy(a, b, sent, received, device_id=across, device_id_type=MESH)

    def share(first, count):
        for zi in range(first, first + count):
            row = r1.at[1 - q, zi]
            whole(row, row, zs1, zr1.at[zi]).wait_recv()
        rows = r1.at[1 - q, pl.ds(first, count)]
        whole(rows, rows, fs, fr).start()

    pl.semaphore_wait(barrier, 8 + 2 + 1 + 15)
    for dz in (4, -4):
        signal(stage, column(dz))

    @pl.when(jnp.logical_not(alone))
    def _():
        spread_one(0, 0)

    lax.fori_loop(1, 8, spread_one, 0)

    @pl.when(alone)
    def _():
        in1[q * 4 + y] = p1[pl.ds(yc * NZ, NZ)]

    for dz in NEAR[:4]:
        along_two(dz).start()
    pl.semaphore_wait(stage, 2)
    signal(opposite_in, opposite)
    for dz in FAR:
        along_two(dz).start()
    met = [whole(p1.at[pl.ds(0, NZ * n)], p1.at[pl.ds(0, NZ * n)], xs, xr) for n in (7, 8)]

    @pl.when(alone)
    def _():
        met[0].wait_recv()

    @pl.when(jnp.logical_not(alone))
    def _():
        met[1].wait_recv()

    s1[...] = in1[0:4] + in1[4:8]
    pl.semaphore_wait(opposite_in, 1)
    for dz in FAR + NEAR + (0,):
        along_one(dz).start()
    for dz in NEAR[4:] + (0,):
        along_two(dz).start()
    spread_two(12, 2)
    spread_two(3, 2)
    spread_two(7, 3)
    spread_two(5, 2)
    spread_two(10, 2)
    share(5, 7)
    share(12, 4)
    share(0, 5)
    spread_two(14, 2)
    spread_two(0, 3)
    r2[pl.ds(yc * NZ, NZ)] = z2[:, yc]

    for copy in loads[5:]:
        copy.wait()
    j = lax.broadcasted_iota(jnp.int32, (G, G), 1)
    hot2 = (((j // 32) * NZ + (z + j % NZ) % NZ) * 2 + (j // NZ) % 2 == i).astype(F32).astype(BF)
    hot1 = (((j % 4) * NZ + (z + (j // 4) % NZ) % NZ) * 2 + j // HALF == i).astype(F32).astype(BF)
    m2s = tuple(dot(v, hot2).astype(BF) for v in split(m2[...]))
    m1s = tuple(dot(v, hot1).astype(BF) for v in split(m1[...]))
    l2s, l1s = split(l2[...]), split(l1[...])

    rows2 = whole(r2.at[pl.ds(0, 7 * NZ)], r2.at[pl.ds(0, 7 * NZ)], send2, recv2)
    shared = whole(r1.at[q], r1.at[q], fs, fr)
    shared.wait_recv()
    for k in range(4):
        w1 = split(dot3(m1s, split(r1[:, :, :, k, :].reshape(G, 128))))
        out[:, 128 * k : 128 * k + 128] = dot3(l1s, w1)
    rows2.wait_recv()
    for k in range(4):
        w2 = split(dot3(m2s, split(r2[:, k, :])))
        out[:, 128 * k : 128 * k + 128] += dot3(l2s, w2)
    whole(s2, s2, zs2, zr2.at[0]).wait_send()
    whole(r1.at[0], r1.at[0], zs1, zr1.at[0]).wait_send()

    @pl.when(alone)
    def _():
        met[0].wait_send()

    @pl.when(jnp.logical_not(alone))
    def _():
        met[1].wait_send()

    rows2.wait_send()
    shared.wait_send()


def on_device(rhs, left_one, left_two, middle_one, middle_two, right_one, right_two, order_one, order_two):
    dma = pltpu.SemaphoreType.DMA
    any_space = pl.BlockSpec(memory_space=pl.ANY)
    return pl.pallas_call(
        kernel,
        out_shape=pltpu.VMEM((256, 512), F32),
        in_specs=[any_space] * 9,
        out_specs=pl.BlockSpec(memory_space=pltpu.VMEM),
        scratch_shapes=[
            pltpu.VMEM((256, 512), F32),
            pltpu.VMEM((256, 128), F32),
            pltpu.VMEM((256, 128), F32),
            pltpu.VMEM((128, 128), F32),
            pltpu.VMEM((128, 128), F32),
            pltpu.VMEM((256, 128), F32),
            pltpu.VMEM((256, 128), F32),
            pltpu.VMEM((1, 128), jnp.int32),
            pltpu.VMEM((1, 128), jnp.int32),
            pltpu.VMEM((G, 4, 128), F32),
            pltpu.VMEM((G, 4, 128), F32),
            pltpu.VMEM((8, NZ, 4, 128), F32),
            pltpu.VMEM((4, NZ, 4, 128), F32),
            pltpu.VMEM((NZ, 8, 4, 128), F32),
            pltpu.VMEM((G, 4, 128), F32),
            pltpu.VMEM((2, NZ, 4, 4, 128), F32),
            dma((9,)), dma, dma((NZ,)), dma, dma, dma, dma((NZ,)), dma, dma, dma, dma,
            pltpu.SemaphoreType.REGULAR,
            pltpu.SemaphoreType.REGULAR,
        ],
        compiler_params=pltpu.CompilerParams(collective_id=0, has_side_effects=True),
        name="butterfly",
    )(rhs, left_one, left_two, middle_one, middle_two, right_one, right_two, order_one, order_two)


def solution(mesh):
    rows = P(("half", "quarter", "grp"), None)
    in_specs = (
        rows, rows, rows,
        P("half", "grp", None, None),
        P(("half", "quarter"), "grp", None, None),
        rows, rows,
        P("half", "grp", None),
        P(("half", "quarter"), "grp", None),
    )
    return jax.shard_map(on_device, mesh=mesh, in_specs=in_specs, out_specs=rows, check_vma=False)
```

time: 46.9 us -> 42.8 us (0.913)
  Pallas kernels: 44.9 us -> 41.9 us
  local copies, waits for them, and re-layouts: 1.87 us -> 0.8 us
    pallas_call x1, Pallas kernels: 44.9 us -> 41.9 us  [on_device(): pl.pallas_call(kernel, out_shape=pltpu.VMEM((256, 512), F32), in_specs=[a...]
    unnamed x1, local copies, waits for them, and re-layouts: 1.87 us -> 0.8 us
where the time goes in v2:
time: 42.8 us; the launch traced here: 42.7 us
  Pallas kernels  41.9 us (98%)
  local copies, waits for them, and re-layouts  0.8 us (2%)
    pallas_call x1, Pallas kernels, on_device(): pl.pallas_call(kernel, out_shape=pltpu.VMEM((256, 512), F32), in_specs=[a...  41.9 us

profile of v2, /device:TPU:1, one launch (start us, length us, event | category | flops | bytes accessed | tf_op | source)
XLA Modules:
  0.0 42.7 jit_solution(1338248404358142505)
XLA Ops:
  0.0 41.9 %butterfly.1 = f32[256,512]{1,0:T(8,128)S(1)} custom-call(f32[256,512]{1,0:T(8,128)} %x_hbm.1, f32[256,128]{1,0:T(8,128)} %l1_hbm.1, f32[256,128]{1,0:T(8,128)} %l2_hbm.1, f32[1,1,128,128]{3,2,1,0:T(8,128)} %m1_hbm.1, f32[1,1,128,128]{3,2,1,0:T(8,128)} %m2_hbm.1, f32[256,128]{1,0:T(8,128)} %rr1_hbm.1, f32[256,128]{1,0:T(8,128)} %rr2_hbm.1, ...), custom_call_target="tpu_custom_call" | custom-call | tf_op jit(solution)/shard_map/butterfly/pallas_call | solution.py:237
  41.9 0.8 %copy.11 = f32[256,512]{1,0:T(8,128)} copy(f32[256,512]{1,0:T(8,128)S(1)} %butterfly.1) | data formatting | bytes 1048576

commit v3 on v2

--- a/solution.py
+++ b/solution.py
@@ -28,6 +28,11 @@
 def dot3(a, b):
     (ah, al), (bh, bl) = a, b
     return dot(ah, bh) + (dot(ah, bl) + dot(al, bh))
+
+
+def deep3(a, b):
+    (ah, al), (bh, bl) = a, b
+    return dot(jnp.concatenate([ah, al], 1), jnp.concatenate([bh, bh], 0)) + dot(ah, bl)
 
 
 def permuted(factor, order, slot):
@@ -163,7 +168,7 @@
     def _():
         in1[q * 4 + y] = p1[pl.ds(yc * NZ, NZ)]
 
-    for dz in NEAR[:4]:
+    for dz in NEAR + (0,):
         along_two(dz).start()
     pl.semaphore_wait(stage, 2)
     signal(opposite_in, opposite)
@@ -183,19 +188,17 @@
     pl.semaphore_wait(opposite_in, 1)
     for dz in FAR + NEAR + (0,):
         along_one(dz).start()
-    for dz in NEAR[4:] + (0,):
-        along_two(dz).start()
-    spread_two(12, 2)
-    spread_two(3, 2)
+    spread_two(12, 4)
+    spread_two(0, 5)
     spread_two(7, 3)
     spread_two(5, 2)
     spread_two(10, 2)
-    share(5, 7)
+    r2[pl.ds(yc * NZ, NZ)] = z2[:, yc]
+    share(7, 3)
+    share(5, 2)
+    share(10, 2)
     share(12, 4)
     share(0, 5)
-    spread_two(14, 2)
-    spread_two(0, 3)
-    r2[pl.ds(yc * NZ, NZ)] = z2[:, yc]
 
     for copy in loads[5:]:
         copy.wait()
@@ -207,15 +210,17 @@
     l2s, l1s = split(l2[...]), split(l1[...])
 
     rows2 = whole(r2.at[pl.ds(0, 7 * NZ)], r2.at[pl.ds(0, 7 * NZ)], send2, recv2)
+    rows2.wait_recv()
+    for k in (0, 2):
+        rows = jnp.concatenate([r2[:, k, :], r2[:, k + 1, :]], 1)
+        w2 = split(deep3(m2s, split(rows)))
+        out[:, 128 * k : 128 * k + 256] = deep3(l2s, w2)
     shared = whole(r1.at[q], r1.at[q], fs, fr)
     shared.wait_recv()
-    for k in range(4):
-        w1 = split(dot3(m1s, split(r1[:, :, :, k, :].reshape(G, 128))))
-        out[:, 128 * k : 128 * k + 128] = dot3(l1s, w1)
-    rows2.wait_recv()
-    for k in range(4):
-        w2 = split(dot3(m2s, split(r2[:, k, :])))
-        out[:, 128 * k : 128 * k + 128] += dot3(l2s, w2)
+    for k in (0, 2):
+        rows = jnp.concatenate([r1[:, :, :, n, :].reshape(G, 128) for n in (k, k + 1)], 1)
+        w1 = split(deep3(m1s, split(rows)))
+        out[:, 128 * k : 128 * k + 256] += deep3(l1s, w1)
     whole(s2, s2, zs2, zr2.at[0]).wait_send()
     whole(r1.at[0], r1.at[0], zs1, zr1.at[0]).wait_send()
 

time: 42.8 us -> 41.2 us (0.963)
  the two profiles are of different devices: /device:TPU:1 before, /device:TPU:2 now
where the time goes in v3:
time: 41.2 us; the launch traced here: 41.1 us
  Pallas kernels  40.3 us (98%)
  local copies, waits for them, and re-layouts  0.8 us (2%)
    pallas_call x1, Pallas kernels, on_device(): pl.pallas_call(kernel, out_shape=pltpu.VMEM((256, 512), F32), in_specs=[a...  40.3 us

profile of v3, /device:TPU:2, one launch (start us, length us, event | category | flops | bytes accessed | tf_op | source)
XLA Modules:
  0.0 41.1 jit_solution(4359897312209407712)
XLA Ops:
  0.0 40.3 %butterfly.1 = f32[256,512]{1,0:T(8,128)S(1)} custom-call(f32[256,512]{1,0:T(8,128)} %x_hbm.1, f32[256,128]{1,0:T(8,128)} %l1_hbm.1, f32[256,128]{1,0:T(8,128)} %l2_hbm.1, f32[1,1,128,128]{3,2,1,0:T(8,128)} %m1_hbm.1, f32[1,1,128,128]{3,2,1,0:T(8,128)} %m2_hbm.1, f32[256,128]{1,0:T(8,128)} %rr1_hbm.1, f32[256,128]{1,0:T(8,128)} %rr2_hbm.1, ...), custom_call_target="tpu_custom_call" | custom-call | tf_op jit(solution)/shard_map/butterfly/pallas_call | solution.py:242
  40.3 0.8 %copy.11 = f32[256,512]{1,0:T(8,128)} copy(f32[256,512]{1,0:T(8,128)S(1)} %butterfly.1) | data formatting | bytes 1048576

commit v4 on v3

--- a/solution.py
+++ b/solution.py
@@ -174,6 +174,8 @@
     signal(opposite_in, opposite)
     for dz in FAR:
         along_two(dz).start()
+    spread_two(12, 4)
+    spread_two(0, 5)
     met = [whole(p1.at[pl.ds(0, NZ * n)], p1.at[pl.ds(0, NZ * n)], xs, xr) for n in (7, 8)]
 
     @pl.when(alone)
@@ -186,19 +188,17 @@
 
     s1[...] = in1[0:4] + in1[4:8]
     pl.semaphore_wait(opposite_in, 1)
-    for dz in FAR + NEAR + (0,):
+    for dz in FAR[:3] + NEAR + (0,) + FAR[3:]:
         along_one(dz).start()
-    spread_two(12, 4)
-    spread_two(0, 5)
     spread_two(7, 3)
     spread_two(5, 2)
     spread_two(10, 2)
     r2[pl.ds(yc * NZ, NZ)] = z2[:, yc]
     share(7, 3)
+    share(12, 4)
+    share(0, 5)
     share(5, 2)
     share(10, 2)
-    share(12, 4)
-    share(0, 5)
 
     for copy in loads[5:]:
         copy.wait()

time: 41.2 us -> 40.4 us (0.981)
  the two profiles are of different devices: /device:TPU:2 before, /device:TPU:1 now
where the time goes in v4:
time: 40.4 us; the launch traced here: 40.2 us
  Pallas kernels  39.4 us (98%)
  local copies, waits for them, and re-layouts  0.8 us (2%)
    pallas_call x1, Pallas kernels, on_device(): pl.pallas_call(kernel, out_shape=pltpu.VMEM((256, 512), F32), in_specs=[a...  39.4 us

profile of v4, /device:TPU:1, one launch (start us, length us, event | category | flops | bytes accessed | tf_op | source)
XLA Modules:
  0.0 40.2 jit_solution(17495500808872843080)
XLA Ops:
  0.0 39.4 %butterfly.1 = f32[256,512]{1,0:T(8,128)S(1)} custom-call(f32[256,512]{1,0:T(8,128)} %x_hbm.1, f32[256,128]{1,0:T(8,128)} %l1_hbm.1, f32[256,128]{1,0:T(8,128)} %l2_hbm.1, f32[1,1,128,128]{3,2,1,0:T(8,128)} %m1_hbm.1, f32[1,1,128,128]{3,2,1,0:T(8,128)} %m2_hbm.1, f32[256,128]{1,0:T(8,128)} %rr1_hbm.1, f32[256,128]{1,0:T(8,128)} %rr2_hbm.1, ...), custom_call_target="tpu_custom_call" | custom-call | tf_op jit(solution)/shard_map/butterfly/pallas_call | solution.py:242
  39.5 0.8 %copy.11 = f32[256,512]{1,0:T(8,128)} copy(f32[256,512]{1,0:T(8,128)S(1)} %butterfly.1) | data formatting | bytes 1048576

commit v5 on v4

--- a/solution.py
+++ b/solution.py
@@ -83,8 +83,7 @@
     across = {"half": h, "quarter": 1 - q, "grp": me}
     opposite = {"half": 1 - h, "quarter": q, "grp": me}
 
-    for copy in loads:
-        copy.start()
+    loads[0].start()
     barrier = pltpu.get_barrier_semaphore()
     for dz in NEAR:
         signal(barrier, sibling(dz))
@@ -94,6 +93,8 @@
     for s in range(1, 16):
         t = (yc * 2 + q + s) % 16
         signal(barrier, {"half": h, "quarter": t % 2, "grp": place(z, t // 2)})
+    for copy in loads[1:]:
+        copy.start()
 
     i = lax.broadcasted_iota(jnp.int32, (G, G), 0)
     slot2 = (((i // 2) % 4) * NZ + i // 8) * 2 + i % 2
@@ -188,17 +189,19 @@
 
     s1[...] = in1[0:4] + in1[4:8]
     pl.semaphore_wait(opposite_in, 1)
-    for dz in FAR[:3] + NEAR + (0,) + FAR[3:]:
+    for dz in FAR[:3] + NEAR[4:] + (0,) + FAR[3:] + NEAR[:4]:
         along_one(dz).start()
     spread_two(7, 3)
     spread_two(5, 2)
     spread_two(10, 2)
     r2[pl.ds(yc * NZ, NZ)] = z2[:, yc]
     share(7, 3)
-    share(12, 4)
-    share(0, 5)
+    share(14, 2)
+    share(0, 3)
     share(5, 2)
     share(10, 2)
+    share(12, 2)
+    share(3, 2)
 
     for copy in loads[5:]:
         copy.wait()

time: 40.4 us -> 40.9 us (1.012)
  the two profiles are of different devices: /device:TPU:1 before, /device:TPU:2 now
where the time goes in v5:
time: 40.9 us; the launch traced here: 40.7 us
  Pallas kernels  39.9 us (98%)
  local copies, waits for them, and re-layouts  0.8 us (2%)
    pallas_call x1, Pallas kernels, on_device(): pl.pallas_call(kernel, out_shape=pltpu.VMEM((256, 512), F32), in_specs=[a...  39.9 us

profile of v5, /device:TPU:2, one launch (start us, length us, event | category | flops | bytes accessed | tf_op | source)
XLA Modules:
  0.0 40.7 jit_solution(12772742840053807233)
XLA Ops:
  0.0 39.9 %butterfly.1 = f32[256,512]{1,0:T(8,128)S(1)} custom-call(f32[256,512]{1,0:T(8,128)} %x_hbm.1, f32[256,128]{1,0:T(8,128)} %l1_hbm.1, f32[256,128]{1,0:T(8,128)} %l2_hbm.1, f32[1,1,128,128]{3,2,1,0:T(8,128)} %m1_hbm.1, f32[1,1,128,128]{3,2,1,0:T(8,128)} %m2_hbm.1, f32[256,128]{1,0:T(8,128)} %rr1_hbm.1, f32[256,128]{1,0:T(8,128)} %rr2_hbm.1, ...), custom_call_target="tpu_custom_call" | custom-call | tf_op jit(solution)/shard_map/butterfly/pallas_call | solution.py:245
  40.0 0.8 %copy.11 = f32[256,512]{1,0:T(8,128)} copy(f32[256,512]{1,0:T(8,128)S(1)} %butterfly.1) | data formatting | bytes 1048576
